TPU v7x, 256 devices: a whole 4x4x8 slice. The times are simulated.
256 devices in a mesh: ctx: 32 (over y, z), tp: 8 (over x, core).
Axes of the slice: x: 4, y: 4, z: 8, core: 2. Of those that a mesh axis runs over, the one named last changes fastest.
Arguments:
- ssm_inputs: bfloat16 [8192, 8192], P('ctx', 'tp'), may hold values from -4 to 4
- state_maps: bfloat16 [8192, 8, 256], P('ctx', 'tp'), may hold values from -4 to 4
- ssm_gates: bfloat16 [8192, 8192], P('ctx', 'tp'), may hold values from -4 to 4
- time_steps: float32 [128, 8192], P('tp', 'ctx'), may hold values from -5 to 512
- log_rates: float32 [128], P('tp'), may hold values from -12 to 1
- skip_gain: float32 [128], P('tp'), may hold values from 0.5 to 2
- conv_inputs: bfloat16 [4, 8192], P(None, 'tp'), may hold values from -3 to 3
- conv_maps: bfloat16 [4, 8, 256], P(None, 'tp'), may hold values from -3 to 3
- norm_gain: float32 [8192], P('tp'), may hold values from 0.1 to 1.9
- out_weight: bfloat16 [8192, 4096], P('tp'), may hold values from -0.0625 to 0.0625
- queries: bfloat16 [8192, 8192], P('ctx', 'tp'), may hold values from -5 to 5
- attention_keys: bfloat16 [8192, 1024], P('ctx', 'tp'), may hold values from -5 to 5
- values: bfloat16 [8192, 1024], P('ctx', 'tp'), may hold values from -4 to 4
Outputs:
- ssm_out: bfloat16 [8192, 4096], P(('ctx', 'tp'))
- attn_out: bfloat16 [8192, 8192], P('ctx', 'tp')
All inputs are finite; a program needn't handle non-finite values.
Results may differ from a plain program's by a relative error of at most 0.03.
Values may be sent and summed in bfloat16 or wider, within the bound.
No kernel may reach another device: no remote copies, remote signals or barrier semaphores. Data moves between devices by JAX's collectives and lax.ppermute only.
A program may use at most 128 MiB of HBM per device.

v0:
```python
import jax
import jax.numpy as jnp
from jax import lax
from jax.sharding import PartitionSpec as P

QUERY_HEADS = 64
KEY_VALUE_HEADS = 8
HEAD_SIZE = 128


def passed_along(shard, axis, by):
    size = lax.axis_size(axis)
    pairs = [(i, i + by) for i in range(size) if 0 <= i + by < size]
    return lax.ppermute(shard, axis, pairs)


def prefix_2(shard, axis, join, neutral):
    place = lax.axis_index(axis)
    gathered = jax.tree.map(
        lambda a, kind: lax.all_gather(a.astype(kind), axis), shard, (jnp.bfloat16, jnp.bfloat16)
    )
    state = jax.tree.map(lambda a, e: jnp.zeros_like(a) + jnp.asarray(e, a.dtype), shard, neutral)

    def one(step, state):
        return join(
            state,
            jax.tree.map(
                lambda a, own: lax.dynamic_index_in_dim(a, step, 0, False).astype(own.dtype),
                gathered,
                shard,
            ),
        )

    return lax.fori_loop(0, place, one, state)


def conv_silu(extended, conv_taps, tok_rows):
    summed = jnp.zeros((tok_rows,) + extended.shape[1:], jnp.float32)
    for tap_index in range(conv_taps.shape[0]):
        summed = summed + conv_taps[tap_index].astype(jnp.float32) * extended[
            tap_index : tap_index + tok_rows
        ].astype(jnp.float32)
    return jax.nn.silu(summed).astype(jnp.bfloat16)


def per_device(
    ssm_inputs,
    state_maps,
    ssm_gates,
    time_steps,
    log_rates,
    skip_gain,
    conv_inputs,
    conv_maps,
    norm_gain,
    out_weight,
    queries,
    attention_keys,
    values,
):
    tok_rows = ssm_inputs.shape[0]
    tap_count = conv_inputs.shape[0]
    groups_here = state_maps.shape[1]
    state_size = state_maps.shape[2] // 2
    heads_here = log_rates.shape[0]
    per_group = heads_here // groups_here
    head_dim = ssm_inputs.shape[1] // heads_here
    my_index = lax.axis_index("ctx")
    lead_inputs, lead_maps = passed_along(
        (ssm_inputs[tok_rows - tap_count + 1 :], state_maps[tok_rows - tap_count + 1 :]), "ctx", 1
    )
    mixed_inputs = conv_silu(
        jnp.concatenate([lead_inputs, ssm_inputs], axis=0), conv_inputs, tok_rows
    )
    mixed_maps = conv_silu(jnp.concatenate([lead_maps, state_maps], axis=0), conv_maps, tok_rows)
    input_heads = mixed_inputs.reshape(tok_rows, groups_here, per_group, head_dim)
    b_maps = mixed_maps[:, :, :state_size]
    c_maps = mixed_maps[:, :, state_size:]
    step_sizes = jax.nn.softplus(time_steps).reshape(groups_here, per_group, tok_rows)
    decline_rate = -jnp.exp(log_rates).reshape(groups_here, per_group)
    running_log = jnp.cumsum(step_sizes * decline_rate[:, :, None], axis=2)
    map_products = jnp.einsum("tgn,sgn->gts", c_maps, b_maps, preferred_element_type=jnp.float32)
    token_location = jnp.arange(tok_rows)
    causal = token_location[:, None] >= token_location[None, :]
    log_gap = running_log[:, :, :, None] - running_log[:, :, None, :]
    decay_table = jnp.where(causal, jnp.exp(jnp.minimum(log_gap, 0.0)), 0.0)
    mixer = (map_products[:, None] * decay_table * step_sizes[:, :, None, :]).astype(jnp.bfloat16)
    inner_part = jnp.einsum(
        "gjts,sgjp->tgjp", mixer, input_heads, preferred_element_type=jnp.float32
    )
    inputs_float = input_heads.astype(jnp.float32)
    tail_weight = jnp.exp(running_log[:, :, -1:] - running_log) * step_sizes
    weighted = (jnp.transpose(tail_weight, (2, 0, 1))[..., None] * inputs_float).astype(
        jnp.bfloat16
    )
    block_state = jnp.einsum("sgjp,sgn->gjpn", weighted, b_maps, preferred_element_type=jnp.float32)
    block_decay = running_log[:, :, -1]

    def combine(earlier, later):
        return (earlier[0] + later[0], jnp.exp(later[0])[:, :, None, None] * earlier[1] + later[1])

    prefix = prefix_2(
        (block_decay, block_state),
        "ctx",
        combine,
        (jnp.zeros_like(block_decay), jnp.zeros_like(block_state)),
    )
    entering = prefix[1]
    carried = jnp.einsum(
        "tgn,gjpn->tgjp", c_maps.astype(jnp.float32), entering, precision=lax.Precision.HIGHEST
    )
    outside = jnp.transpose(jnp.exp(running_log), (2, 0, 1))[..., None] * carried
    ssm_output = (
        inner_part
        + outside
        + skip_gain.reshape(groups_here, per_group)[None, :, :, None] * inputs_float
    )
    channel_count = per_group * head_dim
    gated = ssm_output.reshape(tok_rows, groups_here, channel_count) * jax.nn.silu(
        ssm_gates.reshape(tok_rows, groups_here, channel_count).astype(jnp.float32)
    )
    mean_square = jnp.mean(gated * gated, axis=2, keepdims=True)
    normed = (
        (gated * lax.rsqrt(mean_square + 1e-05)).reshape(tok_rows, groups_here * channel_count)
        * norm_gain
    ).astype(jnp.bfloat16)
    ssm_out = lax.psum_scatter(
        jnp.dot(normed, out_weight, preferred_element_type=jnp.float32).astype(jnp.bfloat16),
        "tp",
        scatter_dimension=0,
        tiled=True,
    )
    kv_heads = attention_keys.shape[1] // HEAD_SIZE
    shared_heads = QUERY_HEADS // KEY_VALUE_HEADS
    score_scale = HEAD_SIZE ** (-0.5)
    query_pos = my_index * tok_rows + token_location
    query_heads = queries.reshape(tok_rows, kv_heads, shared_heads, HEAD_SIZE)
    block_rows = tok_rows // 4
    first_key = jnp.int32(0)
    key_block = lax.all_gather(attention_keys, "ctx", axis=0, tiled=True)
    value_block = lax.all_gather(values, "ctx", axis=0, tiled=True)
    key_count = key_block.shape[0]
    key_head_rows = key_block.reshape(key_count, kv_heads, HEAD_SIZE)
    value_head_rows = value_block.reshape(key_count, kv_heads, HEAD_SIZE)
    key_pos = jnp.arange(key_count)
    peaks = jnp.full((kv_heads, shared_heads, tok_rows), -1e30, jnp.float32)
    totals = jnp.zeros((kv_heads, shared_heads, tok_rows), jnp.float32)
    sums = jnp.zeros((kv_heads, shared_heads, tok_rows, HEAD_SIZE), jnp.float32)
    new_parts = []
    for current_block_index in range(4):
        row_lower = current_block_index * block_rows
        row_upper = row_lower + block_rows
        query_tile_block = query_heads[row_lower:row_upper]
        block_pos = query_pos[row_lower:row_upper]
        old_state = (
            peaks[:, :, row_lower:row_upper],
            totals[:, :, row_lower:row_upper],
            sums[:, :, row_lower:row_upper],
        )

        def update(old_part, query_tile_block=query_tile_block, block_pos=block_pos):
            old_peak, old_total, old_sum = old_part
            scores = (
                jnp.einsum(
                    "bgrd,kgd->grbk",
                    query_tile_block,
                    key_head_rows,
                    preferred_element_type=jnp.float32,
                )
                * score_scale
            )
            allowed = key_pos[None, :] <= block_pos[:, None]
            scores = jnp.where(allowed, scores, -1e30)
            new_peak = jnp.maximum(old_peak, jnp.max(scores, axis=3))
            weights = jnp.where(allowed, jnp.exp(scores - new_peak[..., None]), 0.0)
            new_total = jnp.sum(weights, axis=3)
            new_sum = jnp.einsum(
                "grbk,kgd->grbd",
                weights.astype(jnp.bfloat16),
                value_head_rows,
                preferred_element_type=jnp.float32,
            )
            return (new_peak, new_total, new_sum)

        def unchanged(old_part):
            return old_part

        new_parts.append(
            lax.cond(block_pos[block_rows - 1] >= first_key, update, unchanged, old_state)
        )
    peaks, totals, sums = tuple(
        (
            jnp.concatenate([block_part[member] for block_part in new_parts], axis=2)
            for member in range(3)
        )
    )
    attended = sums / totals[..., None]
    attn_out = (
        jnp.transpose(attended, (2, 0, 1, 3))
        .reshape(tok_rows, kv_heads * shared_heads * HEAD_SIZE)
        .astype(jnp.bfloat16)
    )
    return (ssm_out, attn_out)


def solution(mesh):
    placed = (
        P("ctx", "tp"),
        P("ctx", "tp", None),
        P("ctx", "tp"),
        P("tp", "ctx"),
        P("tp"),
        P("tp"),
        P(None, "tp"),
        P(None, "tp", None),
        P("tp"),
        P("tp", None),
        P("ctx", "tp"),
        P("ctx", "tp"),
        P("ctx", "tp"),
    )
    return jax.shard_map(
        per_device,
        mesh=mesh,
        in_specs=placed,
        out_specs=(P(("ctx", "tp"), None), P("ctx", "tp")),
        check_vma=False,
    )
```

profile of v0, /device:TPU:4, one launch (start us, length us, event | category | flops | bytes accessed | tf_op | source)
XLA Modules:
  0.0 351.8 jit_solution(560110108480496360)
XLA Ops:
  7.2 0.0 all-gather.10.cloned.1.call-start
  7.2 0.7 slice.117
  8.0 0.2 copy.76
  8.2 3.8 %collective-permute-start = (bf16[3,1024]{0,1:T(8,128)(2,1)S(1)}, bf16[3,1024]{0,1:T(8,128)(2,1)S(1)}, u32[]{:S(2)}, u32[]{:S(2)}) collective-permute-start(bf16[3,1024]{0,1:T(8,128)(2,1)S(1)} %copy.76), channel_id=1, source_target_pairs={{0,8},{8,16},{16,24},{24,32},{32,40},{40,48},{48,56},{56,64},{64,7... | collective-permute-start | bytes 18440 | tf_op jit(solution)/shard_map/ppermute | solution.py:14
  12.0 0.7 slice.125
  12.7 3.8 %collective-permute-start.1 = (bf16[3,1,256]{2,0,1:T(4,128)(2,1)S(1)}, bf16[3,1,256]{2,0,1:T(4,128)(2,1)S(1)}, u32[]{:S(2)}, u32[]{:S(2)}) collective-permute-start(bf16[3,1,256]{2,0,1:T(4,128)(2,1)S(1)} %slice.125), channel_id=1, source_target_pairs={{0,8},{8,16},{16,24},{24,32},{32,40},{40,48},{48,56},{56,64},{64,7... | collective-permute-start | bytes 4616 | tf_op jit(solution)/shard_map/ppermute | solution.py:14
  16.5 0.7 exponential_negate_fusion
  17.2 0.8 compare_select_fusion
  18.0 0.6 reduce-window.6
  18.6 0.2 slice_reduce_fusion
  18.8 0.1 copy.83
  19.0 0.1 copy.90
  19.0 0.9 slice_convert_fusion.3
  19.9 0.8 multiply_bitcast_fusion
  20.7 0.8 slice_convert_fusion.7
  21.6 1.2 copy.77
  22.8 1.4 multiply_convert_fusion.7
  24.3 1.5 fusion.96
  25.7 1.0 convolution_convert_fusion.1
  26.8 0.0 all-gather.6.cloned.1.call-start
  26.8 0.7 all-gather.6.cloned.1.call-update
  27.5 0.0 all-gather.8.cloned.1.call-start
  27.6 0.7 all-gather.8.cloned.1.call-update
  28.3 0.0 reduce-scatter.2.cloned.1.call-start
  28.3 40.3 %all-gather = bf16[32,16,1]{1,2,0:T(2,128)(2,1)S(1)} all-gather(bf16[1,16,1]{1,2,0:T(2,128)(2,1)S(1)} %slice.213), channel_id=2, replica_groups=mesh['ctx'=32,'tp'=8] {'ctx'}, dimensions={0}, use_global_device_ids=true | all-gather | bytes 1056 | tf_op jit(solution)/shard_map/all_gather | solution.py:20
  68.7 0.1 copy.85
  68.7 0.1 copy.86
  68.8 0.1 copy.84
  68.9 1.3 copy.88
  70.2 0.2 fusion.107
  70.4 1.4 fusion.87
  71.8 54.2 %all-gather.10.cloned.1.call-done = bf16[512,64,128]{2,1,0:T(8,128)(2,1)} async-done(((bf16[16,64,128]{2,1,0:T(8,128)(2,1)}), bf16[512,64,128]{2,1,0:T(8,128)(2,1)}) %all-gather.10.cloned.1.call-update) | async-done | bytes 8388624 | tf_op jit(solution)/shard_map/all_gather | solution.py:20
  126.0 0.6 fusion.90
  126.6 0.4 multiply_reduce_fusion
  127.0 7.2 %convolution_convert_fusion = bf16[256,4096]{1,0:T(8,128)(2,1)} fusion(bf16[1024,4096]{1,0:T(8,128)(2,1)} %param.32, f32[256,1024]{0,1:T(8,128)S(1)} %get-tuple-element.171, f32[1024]{0:T(1024)S(1)} %copy-done, f32[256]{0:T(256)S(1)} %add_rsqrt_fusion), kind=kOutput, calls=%fused_computation.82 | convolution fusion | flops 2149318656 | bytes 11539456 | tf_op jit(solution)/shard_map/dot_general | solution.py:128
  134.2 0.6 fusion.116
  137.2 66.5 %all-gather.6.cloned.1.call-done = bf16[8192,128]{1,0:T(8,128)(2,1)} async-done(((bf16[256,128]{1,0:T(8,128)(2,1)}), bf16[8192,128]{1,0:T(8,128)(2,1)}) %all-gather.6.cloned.1.call-update) | async-done | bytes 2097168 | tf_op jit(solution)/shard_map/all_gather | solution.py:140
  203.7 77.8 %all-gather.8.cloned.1.call-done = bf16[8192,128]{1,0:T(8,128)(2,1)} async-done(((bf16[256,128]{1,0:T(8,128)(2,1)}), bf16[8192,128]{1,0:T(8,128)(2,1)}) %all-gather.8.cloned.1.call-update) | async-done | bytes 2097168 | tf_op jit(solution)/shard_map/all_gather | solution.py:141
  281.5 15.4 %conditional.4 = (f32[1,8,64]{2,1,0:T(8,128)S(1)}, f32[1,8,64,128]{3,2,1,0:T(8,128)S(1)}) conditional(s32[]{:T(128)} %bitcast.73, () %tuple.48, (s32[8192]{0:T(1024)S(1)}, s32[256]{0:T(256)S(1)}, bf16[8192,1,128]{2,0,1:T(8,128)(2,1)}, bf16[256,1024]{1,0:T(8,128)(2,1)}, bf16[8192,1,128]{2,0,1:T(8,128)(2,1)}) %tuple.109), branch_computations={%region_6.7_spmd, %region_7.10_spmd} | conditional | flops 2202533376 | bytes 65450796 | solution.py:189
  281.5 0.3 broadcast_compare_fusion
  281.8 4.8 %fusion = (f32[8,64]{1,0:T(8,128)S(1)}, f32[8192,64,8]{0,1,2:T(8,128)S(1)}) fusion(pred[64,8192]{1,0:T(8,128)(4,1)S(1)} %broadcast_compare_fusion, bf16[8192,1,128]{2,0,1:T(8,128)(2,1)} %get-tuple-element.97, bf16[256,1024]{1,0:T(8,128)(2,1)} %get-tuple-element.98), kind=kOutput, calls=%fused_computation.4 | convolution fusion | flops 1086324224 | bytes 19531776 | tf_op jit(solution)/shard_map/cond/branch_1_fun/bgrd,kgd->grbk/dot_general | solution.py:164
  286.7 4.7 %fusion.10 = f32[1,8,64,128]{3,2,1,0:T(8,128)S(1)} fusion(bf16[8192,1,128]{2,0,1:T(8,128)(2,1)S(1)} %copy-done.2, f32[8192,64,8]{0,1,2:T(8,128)S(1)} %get-tuple-element.179, f32[8,64]{1,0:T(8,128)S(1)} %broadcast_maximum_fusion, pred[64,8192]{1,0:T(8,128)(4,1)S(1)} %broadcast_compare_fusion), kind=kOutput, calls=%fused_computation.13 | convolution fusion | flops 1094713344 | bytes 19662848 | tf_op jit(solution)/shard_map/cond/branch_1_fun/grbk,kgd->grbd/dot_general | solution.py:177
  291.4 5.5 %fusion.2 = f32[8,64]{1,0:T(8,128)S(1)} fusion(f32[8192,64,8]{0,1,2:T(8,128)S(1)} %get-tuple-element.179, f32[8,64]{1,0:T(8,128)S(1)} %broadcast_maximum_fusion, pred[64,8192]{1,0:T(8,128)(4,1)S(1)} %broadcast_compare_fusion), kind=kLoop, calls=%fused_computation.6 | loop fusion | flops 20971008 | bytes 17305600 | tf_op jit(solution)/shard_map/cond/branch_1_fun/reduce_sum | solution.py:176
  296.9 15.5 %conditional.5 = (f32[1,8,64]{2,1,0:T(8,128)S(1)}, f32[1,8,64,128]{3,2,1,0:T(8,128)S(1)}) conditional(s32[]{:T(128)} %bitcast.76, () %tuple.50, (s32[8192]{0:T(1024)S(1)}, s32[256]{0:T(256)S(1)}, bf16[8192,1,128]{2,0,1:T(8,128)(2,1)}, bf16[256,1024]{1,0:T(8,128)(2,1)}, bf16[8192,1,128]{2,0,1:T(8,128)(2,1)}) %tuple.110), branch_computations={%region_10.11_spmd, %region_11.14_spmd} | conditional | flops 2202533376 | bytes 65450796 | solution.py:189
  296.9 0.1 slice.85
  296.9 0.3 broadcast_compare_fusion.1
  297.3 4.9 %fusion.20 = (f32[8,64]{1,0:T(8,128)S(1)}, f32[8192,64,8]{0,1,2:T(8,128)S(1)}) fusion(pred[64,8192]{1,0:T(8,128)(4,1)S(1)} %broadcast_compare_fusion.1, bf16[8192,1,128]{2,0,1:T(8,128)(2,1)} %get-tuple-element.102, bf16[256,1024]{1,0:T(8,128)(2,1)} %get-tuple-element.103), kind=kOutput, calls=%fused_computation.24 | convolution fusion | flops 1086324224 | bytes 19531776 | tf_op jit(solution)/shard_map/cond/branch_1_fun/bgrd,kgd->grbk/dot_general | solution.py:164
  302.2 4.7 %fusion.30 = f32[1,8,64,128]{3,2,1,0:T(8,128)S(1)} fusion(bf16[8192,1,128]{2,0,1:T(8,128)(2,1)S(1)} %copy-done.3, f32[8192,64,8]{0,1,2:T(8,128)S(1)} %get-tuple-element.181, f32[8,64]{1,0:T(8,128)S(1)} %broadcast_maximum_fusion.1, pred[64,8192]{1,0:T(8,128)(4,1)S(1)} %broadcast_compare_fusion.1), kind=kOutput, calls=%fused_computation.33 | convolution fusion | flops 1094713344 | bytes 19662848 | tf_op jit(solution)/shard_map/cond/branch_1_fun/grbk,kgd->grbd/dot_general | solution.py:177
  306.9 5.5 %fusion.22 = f32[8,64]{1,0:T(8,128)S(1)} fusion(f32[8192,64,8]{0,1,2:T(8,128)S(1)} %get-tuple-element.181, f32[8,64]{1,0:T(8,128)S(1)} %broadcast_maximum_fusion.1, pred[64,8192]{1,0:T(8,128)(4,1)S(1)} %broadcast_compare_fusion.1), kind=kLoop, calls=%fused_computation.26 | loop fusion | flops 20971008 | bytes 17305600 | tf_op jit(solution)/shard_map/cond/branch_1_fun/reduce_sum | solution.py:176
  312.4 15.8 %conditional.6 = (f32[1,8,64]{2,1,0:T(8,128)S(1)}, f32[1,8,64,128]{3,2,1,0:T(8,128)S(1)}) conditional(s32[]{:T(128)} %bitcast.77, () %tuple.51, (s32[8192]{0:T(1024)S(1)}, s32[256]{0:T(256)S(1)}, bf16[8192,1,128]{2,0,1:T(8,128)(2,1)}, bf16[256,1024]{1,0:T(8,128)(2,1)}, bf16[8192,1,128]{2,0,1:T(8,128)(2,1)}) %tuple.111), branch_computations={%region_14.15_spmd, %region_15.18_spmd} | conditional | flops 2202533376 | bytes 65450796 | solution.py:189
  312.6 0.3 broadcast_compare_fusion.2
  312.9 4.9 %fusion.40 = (f32[8,64]{1,0:T(8,128)S(1)}, f32[8192,64,8]{0,1,2:T(8,128)S(1)}) fusion(pred[64,8192]{1,0:T(8,128)(4,1)S(1)} %broadcast_compare_fusion.2, bf16[8192,1,128]{2,0,1:T(8,128)(2,1)} %get-tuple-element.107, bf16[256,1024]{1,0:T(8,128)(2,1)} %get-tuple-element.108), kind=kOutput, calls=%fused_computation.44 | convolution fusion | flops 1086324224 | bytes 19531776 | tf_op jit(solution)/shard_map/cond/branch_1_fun/bgrd,kgd->grbk/dot_general | solution.py:164
  317.8 4.8 %fusion.50 = f32[1,8,64,128]{3,2,1,0:T(8,128)S(1)} fusion(bf16[8192,1,128]{2,0,1:T(8,128)(2,1)S(1)} %copy-done.4, f32[8192,64,8]{0,1,2:T(8,128)S(1)} %get-tuple-element.183, f32[8,64]{1,0:T(8,128)S(1)} %broadcast_maximum_fusion.2, pred[64,8192]{1,0:T(8,128)(4,1)S(1)} %broadcast_compare_fusion.2), kind=kOutput, calls=%fused_computation.53 | convolution fusion | flops 1094713344 | bytes 19662848 | tf_op jit(solution)/shard_map/cond/branch_1_fun/grbk,kgd->grbd/dot_general | solution.py:177
  322.7 5.5 %fusion.42 = f32[8,64]{1,0:T(8,128)S(1)} fusion(f32[8192,64,8]{0,1,2:T(8,128)S(1)} %get-tuple-element.183, f32[8,64]{1,0:T(8,128)S(1)} %broadcast_maximum_fusion.2, pred[64,8192]{1,0:T(8,128)(4,1)S(1)} %broadcast_compare_fusion.2), kind=kLoop, calls=%fused_computation.46 | loop fusion | flops 20971008 | bytes 17305600 | tf_op jit(solution)/shard_map/cond/branch_1_fun/reduce_sum | solution.py:176
  328.1 15.5 %conditional.7 = (f32[1,8,64]{2,1,0:T(8,128)S(1)}, f32[1,8,64,128]{3,2,1,0:T(8,128)S(1)}) conditional(s32[]{:T(128)} %bitcast.78, () %tuple.52, (s32[8192]{0:T(1024)S(1)}, s32[256]{0:T(256)S(1)}, bf16[8192,1,128]{2,0,1:T(8,128)(2,1)}, bf16[256,1024]{1,0:T(8,128)(2,1)}, bf16[8192,1,128]{2,0,1:T(8,128)(2,1)}) %tuple.112), branch_computations={%region_18.19_spmd, %region_19.22_spmd} | conditional | flops 2202533376 | bytes 65450796 | solution.py:189
  328.1 0.1 slice.89
  328.2 0.3 broadcast_compare_fusion.3
  328.6 4.9 %fusion.60 = (f32[8,64]{1,0:T(8,128)S(1)}, f32[8192,64,8]{0,1,2:T(8,128)S(1)}) fusion(pred[64,8192]{1,0:T(8,128)(4,1)S(1)} %broadcast_compare_fusion.3, bf16[8192,1,128]{2,0,1:T(8,128)(2,1)} %get-tuple-element.112, bf16[256,1024]{1,0:T(8,128)(2,1)} %get-tuple-element.113), kind=kOutput, calls=%fused_computation.64 | convolution fusion | flops 1086324224 | bytes 19531776 | tf_op jit(solution)/shard_map/cond/branch_1_fun/bgrd,kgd->grbk/dot_general | solution.py:164
  333.5 4.7 %fusion.70 = f32[1,8,64,128]{3,2,1,0:T(8,128)S(1)} fusion(bf16[8192,1,128]{2,0,1:T(8,128)(2,1)S(1)} %copy-done.5, f32[8192,64,8]{0,1,2:T(8,128)S(1)} %get-tuple-element.185, f32[8,64]{1,0:T(8,128)S(1)} %broadcast_maximum_fusion.3, pred[64,8192]{1,0:T(8,128)(4,1)S(1)} %broadcast_compare_fusion.3), kind=kOutput, calls=%fused_computation.73 | convolution fusion | flops 1094713344 | bytes 19662848 | tf_op jit(solution)/shard_map/cond/branch_1_fun/grbk,kgd->grbd/dot_general | solution.py:177
  338.1 5.5 %fusion.62 = f32[8,64]{1,0:T(8,128)S(1)} fusion(f32[8192,64,8]{0,1,2:T(8,128)S(1)} %get-tuple-element.185, f32[8,64]{1,0:T(8,128)S(1)} %broadcast_maximum_fusion.3, pred[64,8192]{1,0:T(8,128)(4,1)S(1)} %broadcast_compare_fusion.3), kind=kLoop, calls=%fused_computation.66 | loop fusion | flops 20971008 | bytes 17305600 | tf_op jit(solution)/shard_map/cond/branch_1_fun/reduce_sum | solution.py:176
  343.6 0.1 maximum_bitcast_fusion
  343.7 0.4 fusion.102
  344.1 0.3 copy.89
  344.4 0.9 copy.124
  (39 shorter events, 0.3 us)
Async XLA Ops:
  7.2 118.8 %copy-start.1 = (f32[16]{0:T(128)S(1)}, f32[16]{0:T(128)}, u32[]{:S(2)}) copy-start(f32[16]{0:T(128)} %param.28) | copy-start | bytes 196
  7.2 119.8 %copy-start = (f32[1024]{0:T(1024)S(1)}, f32[1024]{0:T(1024)}, u32[]{:S(2)}) copy-start(f32[1024]{0:T(1024)} %param.31) | copy-start | bytes 12292
  7.2 118.7 %all-gather.10.cloned.1.call-start = ((), (), s32[]{:S(2)}) async-start(), calls=%async_computation.4 | async-start | bytes 8650752 | tf_op jit(solution)/shard_map/all_gather | solution.py:20
  8.2 16.1 %collective-permute-start = (bf16[3,1024]{0,1:T(8,128)(2,1)S(1)}, bf16[3,1024]{0,1:T(8,128)(2,1)S(1)}, u32[]{:S(2)}, u32[]{:S(2)}) collective-permute-start(bf16[3,1024]{0,1:T(8,128)(2,1)S(1)} %copy.76), channel_id=1, source_target_pairs={{0,8},{8,16},{16,24},{24,32},{32,40},{40,48},{48,56},{56,64},{64,7... | collective-permute-start | bytes 18440 | tf_op jit(solution)/shard_map/ppermute | solution.py:14
  12.7 10.1 %collective-permute-start.1 = (bf16[3,1,256]{2,0,1:T(4,128)(2,1)S(1)}, bf16[3,1,256]{2,0,1:T(4,128)(2,1)S(1)}, u32[]{:S(2)}, u32[]{:S(2)}) collective-permute-start(bf16[3,1,256]{2,0,1:T(4,128)(2,1)S(1)} %slice.125), channel_id=1, source_target_pairs={{0,8},{8,16},{16,24},{24,32},{32,40},{40,48},{48,56},{56,64},{64,7... | collective-permute-start | bytes 4616 | tf_op jit(solution)/shard_map/ppermute | solution.py:14
  26.8 176.9 %all-gather.6.cloned.1.call-start = ((), (), s32[]{:S(2)}) async-start(), calls=%async_computation.2 | async-start | bytes 2162688 | tf_op jit(solution)/shard_map/all_gather | solution.py:140
  27.5 254.0 %all-gather.8.cloned.1.call-start = ((), (), s32[]{:S(2)}) async-start(), calls=%async_computation.3 | async-start | bytes 2162688 | tf_op jit(solution)/shard_map/all_gather | solution.py:141
  28.3 317.1 %reduce-scatter.2.cloned.1.call-start = ((), (), s32[]{:S(2)}) async-start(), calls=%async_computation.1 | async-start | bytes 2359296 | tf_op jit(solution)/shard_map/reduce_scatter | solution.py:127
  281.5 5.2 %copy-start.2 = (bf16[8192,1,128]{2,0,1:T(8,128)(2,1)S(1)}, bf16[8192,1,128]{2,0,1:T(8,128)(2,1)}, u32[]{:S(2)}) copy-start(bf16[8192,1,128]{2,0,1:T(8,128)(2,1)} %get-tuple-element.99) | copy-start | bytes 6291460 | tf_op jit(solution)/shard_map/cond
  296.9 5.3 %copy-start.3 = (bf16[8192,1,128]{2,0,1:T(8,128)(2,1)S(1)}, bf16[8192,1,128]{2,0,1:T(8,128)(2,1)}, u32[]{:S(2)}) copy-start(bf16[8192,1,128]{2,0,1:T(8,128)(2,1)} %get-tuple-element.104) | copy-start | bytes 6291460 | tf_op jit(solution)/shard_map/cond
  312.6 5.3 %copy-start.4 = (bf16[8192,1,128]{2,0,1:T(8,128)(2,1)S(1)}, bf16[8192,1,128]{2,0,1:T(8,128)(2,1)}, u32[]{:S(2)}) copy-start(bf16[8192,1,128]{2,0,1:T(8,128)(2,1)} %get-tuple-element.109) | copy-start | bytes 6291460 | tf_op jit(solution)/shard_map/cond
  328.1 5.3 %copy-start.5 = (bf16[8192,1,128]{2,0,1:T(8,128)(2,1)S(1)}, bf16[8192,1,128]{2,0,1:T(8,128)(2,1)}, u32[]{:S(2)}) copy-start(bf16[8192,1,128]{2,0,1:T(8,128)(2,1)} %get-tuple-element.114) | copy-start | bytes 6291460 | tf_op jit(solution)/shard_map/cond
Sparse Core Ops, SparseCore 0:
  26.9 98.9 all-gather.9
  128.5 75.1 all-gather.5
  206.3 75.1 all-gather.7
  284.5 28.6 reduce-scatter.1
where the time goes:
time: 353 us; the launch traced here: 352 us
  waiting for transfers between devices  200 us (57%)
  matrix products  48.7 us (14%)
  blocking collectives  40.3 us (11%)
  other arithmetic  31.6 us (9%)
  between operations  16.4 us (5%)
  starting transfers between devices  7.79 us (2%)
  local copies, waits for them, and re-layouts  6.81 us (2%)
    all_gather x1, waiting for transfers between devices, per_device(): value_block = lax.all_gather(values, 'ctx', axis=0, tiled=True)  77.8 us
    all_gather x1, waiting for transfers between devices, per_device(): key_block = lax.all_gather(attention_keys, 'ctx', axis=0, tiled=True)  66.5 us
    all_gather x1, waiting for transfers between devices, prefix_2(): lax.all_gather(a.astype(kind), axis)  54.2 us
    all_gather x1, blocking collectives, prefix_2(): lax.all_gather(a.astype(kind), axis)  40.3 us
    reduce_sum x4, other arithmetic, update(): new_total = jnp.sum(weights, axis=3)  21.9 us
    dot_general x4, matrix products, update(): jnp.einsum('bgrd,kgd->grbk', query_tile_block, key_head_rows, preferred_e...  19.5 us
    dot_general x4, matrix products, update(): jnp.einsum('grbk,kgd->grbd', weights.astype(jnp.bfloat16), value_head_row...  18.8 us
    ppermute x2, starting transfers between devices, passed_along(): return lax.ppermute(shard, axis, pairs)  7.64 us
  transfers between devices with their start and end apart: 6, of which 3 were waited for; matrix products, arithmetic and copies ran while one was open for 24% of the time, Pallas kernels for 0%

commit v1 on v0

--- a/solution.py
+++ b/solution.py
@@ -137,8 +137,13 @@
     query_heads = queries.reshape(tok_rows, kv_heads, shared_heads, HEAD_SIZE)
     block_rows = tok_rows // 4
     first_key = jnp.int32(0)
-    key_block = lax.all_gather(attention_keys, "ctx", axis=0, tiled=True)
-    value_block = lax.all_gather(values, "ctx", axis=0, tiled=True)
+    key_block, value_block = jnp.split(
+        lax.all_gather(
+            jnp.concatenate([attention_keys, values], axis=1), "ctx", axis=0, tiled=True
+        ),
+        [attention_keys.shape[1]],
+        axis=1,
+    )
     key_count = key_block.shape[0]
     key_head_rows = key_block.reshape(key_count, kv_heads, HEAD_SIZE)
     value_head_rows = value_block.reshape(key_count, kv_heads, HEAD_SIZE)

time: 353 us -> 284 us (0.80)
  waiting for transfers between devices: 200 us -> 125 us
  local copies, waits for them, and re-layouts: 6.81 us -> 10.6 us
    all_gather x2 -> x1, waiting for transfers between devices: 144 us -> 70.7 us  [per_device(): lax.all_gather(jnp.concatenate([attention_keys, values], axis=1), 'ctx',...]
    reshape x2 -> x3, local copies, waits for them, and re-layouts: 0.02 us -> 3.81 us  [the longest x1 3.79 us: per_device(): value_head_rows = value_block.reshape(key_count, kv_heads, HEAD_SIZE)]
  transfers between devices with their start and end apart: 6 -> 5, of which waited for: 3 -> 2; matrix products, arithmetic and copies ran while one was open for 24% -> 32% of each run, Pallas kernels for 0% -> 0%
where the time goes in v1:
time: 284 us; the launch traced here: 282 us
  waiting for transfers between devices  125 us (44%)
  matrix products  48.6 us (17%)
  blocking collectives  40.3 us (14%)
  other arithmetic  33.2 us (12%)
  between operations  16.4 us (6%)
  local copies, waits for them, and re-layouts  10.6 us (4%)
  starting transfers between devices  7.76 us (3%)
    all_gather x1, waiting for transfers between devices, per_device(): lax.all_gather(jnp.concatenate([attention_keys, values], axis=1), 'ctx',...  70.7 us
    all_gather x1, waiting for transfers between devices, prefix_2(): lax.all_gather(a.astype(kind), axis)  54.1 us
    all_gather x1, blocking collectives, prefix_2(): lax.all_gather(a.astype(kind), axis)  40.3 us
    reduce_sum x4, other arithmetic, update(): new_total = jnp.sum(weights, axis=3)  21.9 us
    dot_general x4, matrix products, update(): jnp.einsum('grbk,kgd->grbd', weights.astype(jnp.bfloat16), value_head_row...  19.6 us
    dot_general x4, matrix products, update(): jnp.einsum('bgrd,kgd->grbk', query_tile_block, key_head_rows, preferred_e...  18.6 us
    ppermute x2, starting transfers between devices, passed_along(): return lax.ppermute(shard, axis, pairs)  7.64 us
    dot_general x1, matrix products, per_device(): jnp.dot(normed, out_weight, preferred_element_type=jnp.float32)  7.2 us
  transfers between devices with their start and end apart: 5, of which 2 were waited for; matrix products, arithmetic and copies ran while one was open for 32% of the time, Pallas kernels for 0%

profile of v1, /device:TPU:4, one launch (start us, length us, event | category | flops | bytes accessed | tf_op | source)
XLA Modules:
  0.0 282.3 jit_solution(7875068852998543862)
XLA Ops:
  7.2 0.0 all-gather.7.cloned.1.call-start
  7.2 0.7 slice.117
  8.0 0.2 copy.76
  8.2 3.8 %collective-permute-start = (bf16[3,1024]{0,1:T(8,128)(2,1)S(1)}, bf16[3,1024]{0,1:T(8,128)(2,1)S(1)}, u32[]{:S(2)}, u32[]{:S(2)}) collective-permute-start(bf16[3,1024]{0,1:T(8,128)(2,1)S(1)} %copy.76), channel_id=1, source_target_pairs={{0,8},{8,16},{16,24},{24,32},{32,40},{40,48},{48,56},{56,64},{64,7... | collective-permute-start | bytes 18440 | tf_op jit(solution)/shard_map/ppermute | solution.py:14
  12.0 0.7 slice.125
  12.7 3.8 %collective-permute-start.1 = (bf16[3,1,256]{2,0,1:T(4,128)(2,1)S(1)}, bf16[3,1,256]{2,0,1:T(4,128)(2,1)S(1)}, u32[]{:S(2)}, u32[]{:S(2)}) collective-permute-start(bf16[3,1,256]{2,0,1:T(4,128)(2,1)S(1)} %slice.125), channel_id=1, source_target_pairs={{0,8},{8,16},{16,24},{24,32},{32,40},{40,48},{48,56},{56,64},{64,7... | collective-permute-start | bytes 4616 | tf_op jit(solution)/shard_map/ppermute | solution.py:14
  16.5 0.7 exponential_negate_fusion
  17.2 0.8 compare_select_fusion
  18.0 0.6 reduce-window.6
  18.6 0.2 slice_reduce_fusion
  18.8 0.1 copy.83
  19.0 0.1 copy.90
  19.0 0.9 slice_convert_fusion.3
  19.9 0.8 multiply_bitcast_fusion
  20.7 0.8 slice_convert_fusion.7
  21.6 1.2 copy.77
  22.8 1.4 multiply_convert_fusion.7
  24.3 1.5 fusion.96
  25.7 1.0 convolution_convert_fusion.1
  26.8 0.0 all-gather.5.cloned.1.call-start
  26.8 1.5 pad_maximum_fusion.2
  28.4 0.0 all-gather.5.cloned.1.call-update
  28.4 0.0 reduce-scatter.2.cloned.1.call-start
  28.5 40.3 %all-gather = bf16[32,16,1]{1,2,0:T(2,128)(2,1)S(1)} all-gather(bf16[1,16,1]{1,2,0:T(2,128)(2,1)S(1)} %slice.213), channel_id=2, replica_groups=mesh['ctx'=32,'tp'=8] {'ctx'}, dimensions={0}, use_global_device_ids=true | all-gather | bytes 1056 | tf_op jit(solution)/shard_map/all_gather | solution.py:20
  68.8 0.1 copy.85
  68.9 0.1 copy.86
  69.0 0.1 copy.84
  69.0 1.2 copy.88
  70.3 0.2 fusion.107
  70.5 1.4 fusion.87
  71.9 54.1 %all-gather.7.cloned.1.call-done = bf16[512,64,128]{2,1,0:T(8,128)(2,1)} async-done(((bf16[16,64,128]{2,1,0:T(8,128)(2,1)}), bf16[512,64,128]{2,1,0:T(8,128)(2,1)}) %all-gather.7.cloned.1.call-update) | async-done | bytes 8388624 | tf_op jit(solution)/shard_map/all_gather | solution.py:20
  126.1 0.6 fusion.90
  126.7 0.4 multiply_reduce_fusion
  127.1 7.2 %convolution_convert_fusion = bf16[256,4096]{1,0:T(8,128)(2,1)} fusion(bf16[1024,4096]{1,0:T(8,128)(2,1)} %param.32, f32[256,1024]{0,1:T(8,128)S(1)} %get-tuple-element.171, f32[1024]{0:T(1024)S(1)} %copy-done, f32[256]{0:T(256)S(1)} %add_rsqrt_fusion), kind=kOutput, calls=%fused_computation.82 | convolution fusion | flops 2149318656 | bytes 11539456 | tf_op jit(solution)/shard_map/dot_general | solution.py:128
  134.3 0.0 reduce-scatter.2.cloned.1.call-update
  134.4 0.6 fusion.116
  137.4 70.7 %all-gather.5.cloned.1.call-done = bf16[8192,256]{1,0:T(8,128)(2,1)} async-done(((bf16[256,256]{1,0:T(8,128)(2,1)}), bf16[8192,256]{1,0:T(8,128)(2,1)}) %all-gather.5.cloned.1.call-update) | async-done | bytes 4194320 | tf_op jit(solution)/shard_map/all_gather | solution.py:141
  208.1 3.8 %slice_bitcast_fusion.4 = (bf16[8192,1,128]{2,0,1:T(8,128)(2,1)S(1)}, bf16[8192,1,128]{2,0,1:T(8,128)(2,1)}) fusion(bf16[8192,256]{1,0:T(8,128)(2,1)} %all-gather.5.cloned.1.call-done), kind=kLoop, calls=%fused_computation.85 | loop fusion | bytes 8388608 | tf_op jit(solution)/shard_map/reshape | solution.py:149
  211.9 15.6 %conditional.4 = (f32[1,8,64]{2,1,0:T(8,128)S(1)}, f32[1,8,64,128]{3,2,1,0:T(8,128)S(1)}) conditional(s32[]{:T(128)} %bitcast.73, () %tuple.48, (s32[8192]{0:T(1024)S(1)}, s32[256]{0:T(256)S(1)}, bf16[8192,1,128]{2,0,1:T(8,128)(2,1)}, bf16[256,1024]{1,0:T(8,128)(2,1)S(1)}, bf16[8192,1,128]{2,0,1:T(8,128)(2,1)S(1)}) %tuple.104), branch_computations={%region_6.7_spmd, %region_7.10_spmd} | conditional | flops 2202533376 | bytes 57062160 | solution.py:194
  212.1 0.3 broadcast_compare_fusion
  212.4 4.6 %fusion = (f32[8,64]{1,0:T(8,128)S(1)}, f32[8192,64,8]{0,1,2:T(8,128)S(1)}) fusion(pred[64,8192]{1,0:T(8,128)(4,1)S(1)} %broadcast_compare_fusion, bf16[8192,1,128]{2,0,1:T(8,128)(2,1)} %get-tuple-element.97, bf16[256,1024]{1,0:T(8,128)(2,1)S(1)} %get-tuple-element.98), kind=kOutput, calls=%fused_computation.4 | convolution fusion | flops 1086324224 | bytes 19531776 | tf_op jit(solution)/shard_map/cond/branch_1_fun/bgrd,kgd->grbk/dot_general | solution.py:169
  217.1 4.9 %fusion.10 = f32[1,8,64,128]{3,2,1,0:T(8,128)S(1)} fusion(bf16[8192,1,128]{2,0,1:T(8,128)(2,1)S(1)} %get-tuple-element.99, f32[8192,64,8]{0,1,2:T(8,128)S(1)} %get-tuple-element.179, f32[8,64]{1,0:T(8,128)S(1)} %broadcast_maximum_fusion, pred[64,8192]{1,0:T(8,128)(4,1)S(1)} %broadcast_compare_fusion), kind=kOutput, calls=%fused_computation.13 | convolution fusion | flops 1094713344 | bytes 19662848 | tf_op jit(solution)/shard_map/cond/branch_1_fun/grbk,kgd->grbd/dot_general | solution.py:182
  222.0 5.5 %fusion.2 = f32[8,64]{1,0:T(8,128)S(1)} fusion(f32[8192,64,8]{0,1,2:T(8,128)S(1)} %get-tuple-element.179, f32[8,64]{1,0:T(8,128)S(1)} %broadcast_maximum_fusion, pred[64,8192]{1,0:T(8,128)(4,1)S(1)} %broadcast_compare_fusion), kind=kLoop, calls=%fused_computation.6 | loop fusion | flops 20971008 | bytes 17305600 | tf_op jit(solution)/shard_map/cond/branch_1_fun/reduce_sum | solution.py:181
  227.5 15.5 %conditional.5 = (f32[1,8,64]{2,1,0:T(8,128)S(1)}, f32[1,8,64,128]{3,2,1,0:T(8,128)S(1)}) conditional(s32[]{:T(128)} %bitcast.76, () %tuple.50, (s32[8192]{0:T(1024)S(1)}, s32[256]{0:T(256)S(1)}, bf16[8192,1,128]{2,0,1:T(8,128)(2,1)}, bf16[256,1024]{1,0:T(8,128)(2,1)S(1)}, bf16[8192,1,128]{2,0,1:T(8,128)(2,1)S(1)}) %tuple.105), branch_computations={%region_10.11_spmd, %region_11.14_spmd} | conditional | flops 2202533376 | bytes 57062160 | solution.py:194
  227.5 0.1 slice.85
  227.5 0.3 broadcast_compare_fusion.1
  227.9 4.7 %fusion.20 = (f32[8,64]{1,0:T(8,128)S(1)}, f32[8192,64,8]{0,1,2:T(8,128)S(1)}) fusion(pred[64,8192]{1,0:T(8,128)(4,1)S(1)} %broadcast_compare_fusion.1, bf16[8192,1,128]{2,0,1:T(8,128)(2,1)} %get-tuple-element.102, bf16[256,1024]{1,0:T(8,128)(2,1)S(1)} %get-tuple-element.103), kind=kOutput, calls=%fused_computation.24 | convolution fusion | flops 1086324224 | bytes 19531776 | tf_op jit(solution)/shard_map/cond/branch_1_fun/bgrd,kgd->grbk/dot_general | solution.py:169
  232.6 4.9 %fusion.30 = f32[1,8,64,128]{3,2,1,0:T(8,128)S(1)} fusion(bf16[8192,1,128]{2,0,1:T(8,128)(2,1)S(1)} %get-tuple-element.104, f32[8192,64,8]{0,1,2:T(8,128)S(1)} %get-tuple-element.181, f32[8,64]{1,0:T(8,128)S(1)} %broadcast_maximum_fusion.1, pred[64,8192]{1,0:T(8,128)(4,1)S(1)} %broadcast_compare_fusion.1), kind=kOutput, calls=%fused_computation.33 | convolution fusion | flops 1094713344 | bytes 19662848 | tf_op jit(solution)/shard_map/cond/branch_1_fun/grbk,kgd->grbd/dot_general | solution.py:182
  237.5 5.5 %fusion.22 = f32[8,64]{1,0:T(8,128)S(1)} fusion(f32[8192,64,8]{0,1,2:T(8,128)S(1)} %get-tuple-element.181, f32[8,64]{1,0:T(8,128)S(1)} %broadcast_maximum_fusion.1, pred[64,8192]{1,0:T(8,128)(4,1)S(1)} %broadcast_compare_fusion.1), kind=kLoop, calls=%fused_computation.26 | loop fusion | flops 20971008 | bytes 17305600 | tf_op jit(solution)/shard_map/cond/branch_1_fun/reduce_sum | solution.py:181
  242.9 15.6 %conditional.6 = (f32[1,8,64]{2,1,0:T(8,128)S(1)}, f32[1,8,64,128]{3,2,1,0:T(8,128)S(1)}) conditional(s32[]{:T(128)} %bitcast.77, () %tuple.51, (s32[8192]{0:T(1024)S(1)}, s32[256]{0:T(256)S(1)}, bf16[8192,1,128]{2,0,1:T(8,128)(2,1)}, bf16[256,1024]{1,0:T(8,128)(2,1)S(1)}, bf16[8192,1,128]{2,0,1:T(8,128)(2,1)S(1)}) %tuple.106), branch_computations={%region_14.15_spmd, %region_15.18_spmd} | conditional | flops 2202533376 | bytes 57062160 | solution.py:194
  243.1 0.3 broadcast_compare_fusion.2
  243.5 4.7 %fusion.40 = (f32[8,64]{1,0:T(8,128)S(1)}, f32[8192,64,8]{0,1,2:T(8,128)S(1)}) fusion(pred[64,8192]{1,0:T(8,128)(4,1)S(1)} %broadcast_compare_fusion.2, bf16[8192,1,128]{2,0,1:T(8,128)(2,1)} %get-tuple-element.107, bf16[256,1024]{1,0:T(8,128)(2,1)S(1)} %get-tuple-element.108), kind=kOutput, calls=%fused_computation.44 | convolution fusion | flops 1086324224 | bytes 19531776 | tf_op jit(solution)/shard_map/cond/branch_1_fun/bgrd,kgd->grbk/dot_general | solution.py:169
  248.2 4.9 %fusion.50 = f32[1,8,64,128]{3,2,1,0:T(8,128)S(1)} fusion(bf16[8192,1,128]{2,0,1:T(8,128)(2,1)S(1)} %get-tuple-element.109, f32[8192,64,8]{0,1,2:T(8,128)S(1)} %get-tuple-element.183, f32[8,64]{1,0:T(8,128)S(1)} %broadcast_maximum_fusion.2, pred[64,8192]{1,0:T(8,128)(4,1)S(1)} %broadcast_compare_fusion.2), kind=kOutput, calls=%fused_computation.53 | convolution fusion | flops 1094713344 | bytes 19662848 | tf_op jit(solution)/shard_map/cond/branch_1_fun/grbk,kgd->grbd/dot_general | solution.py:182
  253.1 5.5 %fusion.42 = f32[8,64]{1,0:T(8,128)S(1)} fusion(f32[8192,64,8]{0,1,2:T(8,128)S(1)} %get-tuple-element.183, f32[8,64]{1,0:T(8,128)S(1)} %broadcast_maximum_fusion.2, pred[64,8192]{1,0:T(8,128)(4,1)S(1)} %broadcast_compare_fusion.2), kind=kLoop, calls=%fused_computation.46 | loop fusion | flops 20971008 | bytes 17305600 | tf_op jit(solution)/shard_map/cond/branch_1_fun/reduce_sum | solution.py:181
  258.6 15.5 %conditional.7 = (f32[1,8,64]{2,1,0:T(8,128)S(1)}, f32[1,8,64,128]{3,2,1,0:T(8,128)S(1)}) conditional(s32[]{:T(128)} %bitcast.78, () %tuple.52, (s32[8192]{0:T(1024)S(1)}, s32[256]{0:T(256)S(1)}, bf16[8192,1,128]{2,0,1:T(8,128)(2,1)}, bf16[256,1024]{1,0:T(8,128)(2,1)S(1)}, bf16[8192,1,128]{2,0,1:T(8,128)(2,1)S(1)}) %tuple.107), branch_computations={%region_18.19_spmd, %region_19.22_spmd} | conditional | flops 2202533376 | bytes 57062160 | solution.py:194
  258.6 0.1 slice.89
  258.7 0.3 broadcast_compare_fusion.3
  259.0 4.6 %fusion.60 = (f32[8,64]{1,0:T(8,128)S(1)}, f32[8192,64,8]{0,1,2:T(8,128)S(1)}) fusion(pred[64,8192]{1,0:T(8,128)(4,1)S(1)} %broadcast_compare_fusion.3, bf16[8192,1,128]{2,0,1:T(8,128)(2,1)} %get-tuple-element.112, bf16[256,1024]{1,0:T(8,128)(2,1)S(1)} %get-tuple-element.113), kind=kOutput, calls=%fused_computation.64 | convolution fusion | flops 1086324224 | bytes 19531776 | tf_op jit(solution)/shard_map/cond/branch_1_fun/bgrd,kgd->grbk/dot_general | solution.py:169
  263.7 4.9 %fusion.70 = f32[1,8,64,128]{3,2,1,0:T(8,128)S(1)} fusion(bf16[8192,1,128]{2,0,1:T(8,128)(2,1)S(1)} %get-tuple-element.114, f32[8192,64,8]{0,1,2:T(8,128)S(1)} %get-tuple-element.185, f32[8,64]{1,0:T(8,128)S(1)} %broadcast_maximum_fusion.3, pred[64,8192]{1,0:T(8,128)(4,1)S(1)} %broadcast_compare_fusion.3), kind=kOutput, calls=%fused_computation.73 | convolution fusion | flops 1094713344 | bytes 19662848 | tf_op jit(solution)/shard_map/cond/branch_1_fun/grbk,kgd->grbd/dot_general | solution.py:182
  268.6 5.5 %fusion.62 = f32[8,64]{1,0:T(8,128)S(1)} fusion(f32[8192,64,8]{0,1,2:T(8,128)S(1)} %get-tuple-element.185, f32[8,64]{1,0:T(8,128)S(1)} %broadcast_maximum_fusion.3, pred[64,8192]{1,0:T(8,128)(4,1)S(1)} %broadcast_compare_fusion.3), kind=kLoop, calls=%fused_computation.66 | loop fusion | flops 20971008 | bytes 17305600 | tf_op jit(solution)/shard_map/cond/branch_1_fun/reduce_sum | solution.py:181
  274.1 0.1 maximum_bitcast_fusion
  274.1 0.4 fusion.102
  274.5 0.3 copy.89
  274.8 0.9 copy.124
  (32 shorter events, 0.3 us)
Async XLA Ops:
  7.2 118.9 %copy-start.1 = (f32[16]{0:T(128)S(1)}, f32[16]{0:T(128)}, u32[]{:S(2)}) copy-start(f32[16]{0:T(128)} %param.28) | copy-start | bytes 196
  7.2 119.9 %copy-start = (f32[1024]{0:T(1024)S(1)}, f32[1024]{0:T(1024)}, u32[]{:S(2)}) copy-start(f32[1024]{0:T(1024)} %param.31) | copy-start | bytes 12292
  7.2 118.8 %all-gather.7.cloned.1.call-start = ((), (), s32[]{:S(2)}) async-start(), calls=%async_computation.3 | async-start | bytes 8650752 | tf_op jit(solution)/shard_map/all_gather | solution.py:20
  8.2 16.1 %collective-permute-start = (bf16[3,1024]{0,1:T(8,128)(2,1)S(1)}, bf16[3,1024]{0,1:T(8,128)(2,1)S(1)}, u32[]{:S(2)}, u32[]{:S(2)}) collective-permute-start(bf16[3,1024]{0,1:T(8,128)(2,1)S(1)} %copy.76), channel_id=1, source_target_pairs={{0,8},{8,16},{16,24},{24,32},{32,40},{40,48},{48,56},{56,64},{64,7... | collective-permute-start | bytes 18440 | tf_op jit(solution)/shard_map/ppermute | solution.py:14
  12.7 10.1 %collective-permute-start.1 = (bf16[3,1,256]{2,0,1:T(4,128)(2,1)S(1)}, bf16[3,1,256]{2,0,1:T(4,128)(2,1)S(1)}, u32[]{:S(2)}, u32[]{:S(2)}) collective-permute-start(bf16[3,1,256]{2,0,1:T(4,128)(2,1)S(1)} %slice.125), channel_id=1, source_target_pairs={{0,8},{8,16},{16,24},{24,32},{32,40},{40,48},{48,56},{56,64},{64,7... | collective-permute-start | bytes 4616 | tf_op jit(solution)/shard_map/ppermute | solution.py:14
  26.8 181.3 %all-gather.5.cloned.1.call-start = ((), (), s32[]{:S(2)}) async-start(), calls=%async_computation.2 | async-start | bytes 4325376 | tf_op jit(solution)/shard_map/all_gather | solution.py:141
  28.4 247.3 %reduce-scatter.2.cloned.1.call-start = ((), (), s32[]{:S(2)}) async-start(), calls=%async_computation.1 | async-start | bytes 2359296 | tf_op jit(solution)/shard_map/reduce_scatter | solution.py:127
  126.1 85.8 %copy-start.2 = (bf16[256,1024]{1,0:T(8,128)(2,1)S(1)}, bf16[256,1024]{1,0:T(8,128)(2,1)}, u32[]{:S(2)}) copy-start(bf16[256,1024]{1,0:T(8,128)(2,1)} %param.33) | copy-start | bytes 1572868
Sparse Core Ops, SparseCore 0:
  26.9 99.0 all-gather.6
  129.2 78.8 all-gather.4
  211.2 28.2 reduce-scatter.1
